TPU v7x, 256 devices: a whole 4x4x8 slice. The times are simulated.
256 devices in a mesh: band: 8 (over y, core), plane: 32 (over x, z).
Axes of the slice: x: 4, y: 4, z: 8, core: 2. Of those that a mesh axis runs over, the one named last changes fastest.
Arguments:
- psi: float32 [2, 8, 4096, 128], P(None, 'band', 'plane'), may hold values from -8 to 8
- potential: float32 [96, 9216], P('plane'), may hold values from 0 to 2
- stick_column: int32 [4096], P('plane'), may hold values from 0 to 9215, as said below
- stick_length: int32 [4096], P('plane'), may hold values from 0 to 49, as said below
Outputs:
- psi_new: float32 [2, 8, 4096, 128], P(None, 'band', 'plane')
- potential_new: float32 [96, 9216], P('plane')
Inputs may be any that keep to these rules, and one draw needn't show every extreme that they name: `stick_column`: within each device's block of 128 slots the live sticks come first and the other slots are empty with column 0. Over all devices the live slots hold every column (mx mod 96) * 96 + (my mod 96) with mx * mx + my * my <= 576 exactly once, in an order drawn from the seed; some device's block is full and the others hold fewer. `stick_length`: A live slot's length is 2 h + 1, with h the largest whole number such that mx * mx + my * my + h * h <= 576 for its column; empty slots have length 0.
All inputs are finite; a program needn't handle non-finite values.
Results may differ from a plain program's by a relative error of at most 0.0001.
Values sent between devices are 32-bit elements; how exact they have to be, the bound alone decides.
No kernel may reach another device: no remote copies, remote signals or barrier semaphores. Data moves between devices by JAX's collectives and lax.ppermute only.
A program may use at most 64 MiB of HBM per device.

v0:
```python
import math
import jax
import jax.numpy as jnp
from jax import lax
from jax.sharding import PartitionSpec as P

NG = 96
RAD = 24
STICK_COEFFS = 128
BAND_DEV = 1
HIGHEST = lax.Precision.HIGHEST
TIMESTEP = 0.6
LINEAR_GAIN = 0.5
CUBIC_GAIN = 0.3


def turning(values):
    return values.astype(jnp.float32) * (2.0 * math.pi / NG)


def height_tables(lengths, columns, planes, device_list):
    order = jnp.arange(STICK_COEFFS, dtype=jnp.int32)
    height = (
        jnp.arange(device_list, dtype=jnp.int32)[None, :] * planes
        + jnp.arange(planes, dtype=jnp.int32)[:, None]
    )
    scale = NG ** (-0.5)
    wave_angle = turning(order[:, None, None] * height[None, :, :] % NG)
    wave = (jnp.cos(wave_angle) * scale, jnp.sin(wave_angle) * scale)
    half = (lengths - 1) // 2
    shift_angle = -turning(height[:, :, None] * half[None, None, :] % NG)
    shift = (jnp.cos(shift_angle), jnp.sin(shift_angle))
    mask = (order[None, :] < lengths[:, None]).astype(jnp.float32)
    first = columns // NG
    second = columns % NG
    first = jnp.where(first > NG // 2, first - NG, first)
    second = jnp.where(second > NG // 2, second - NG, second)
    depth = order[None, :] - half[:, None]
    kinetic = (
        ((first * first + second * second)[:, None] + depth * depth).astype(jnp.float32)
        / (RAD * RAD)
        * mask
    )
    return (wave, shift, mask, kinetic)


def along_height(terms, tables):
    wave, shift = (tables[0], tables[1])

    def contract(left, right):
        return jnp.einsum("bsj,jdn->bdns", left, right, precision=HIGHEST)

    upper_real = contract(terms[0], wave[0]) - contract(terms[1], wave[1])
    upper_imag = contract(terms[0], wave[1]) + contract(terms[1], wave[0])
    return jnp.stack(
        [
            upper_real * shift[0] - upper_imag * shift[1],
            upper_real * shift[1] + upper_imag * shift[0],
        ]
    )


def from_height(values, tables):
    wave, shift, mask = (tables[0], tables[1], tables[2])
    turned_real = values[0] * shift[0] + values[1] * shift[1]
    turned_imag = values[1] * shift[0] - values[0] * shift[1]

    def contract(left, right):
        return jnp.einsum("bdns,jdn->bsj", left, right, precision=HIGHEST)

    real_part = contract(turned_real, wave[0]) + contract(turned_imag, wave[1])
    imag_part = contract(turned_imag, wave[0]) - contract(turned_real, wave[1])
    return jnp.stack([real_part * mask, imag_part * mask])


def plane_tables():
    index = jnp.arange(NG, dtype=jnp.int32)
    angle = turning(index[:, None] * index[None, :] % NG)
    scale = NG ** (-0.5)
    return (jnp.cos(angle) * scale, jnp.sin(angle) * scale)


def plane_transform(values, cosine, sine):
    bands, planes = (values.shape[1], values.shape[2])
    real_part = values[0].reshape(bands, planes, NG, NG)
    imag_part = values[1].reshape(bands, planes, NG, NG)

    def inner(left, right):
        return jnp.einsum("bdmk,ky->bdmy", left, right, precision=HIGHEST)

    def outer(left, right):
        return jnp.einsum("mx,bdmy->bdxy", left, right, precision=HIGHEST)

    middle_real = inner(real_part, cosine) - inner(imag_part, sine)
    middle_imag = inner(real_part, sine) + inner(imag_part, cosine)
    final_real = outer(cosine, middle_real) - outer(sine, middle_imag)
    final_imag = outer(sine, middle_real) + outer(cosine, middle_imag)
    return jnp.stack([final_real, final_imag]).reshape(2, bands, planes, NG * NG)


def cell_slots(columns, lengths):
    count = columns.shape[0]
    target = jnp.where(lengths > 0, columns, NG * NG)
    table = jnp.full((NG * NG,), -1, jnp.int32)
    return table.at[target].set(jnp.arange(count, dtype=jnp.int32), mode="drop")


def spread_columns(values, table):
    picked = jnp.take(values, jnp.maximum(table, 0), axis=3)
    return jnp.where(table >= 0, picked, 0.0)


def modulus(field):
    return jnp.sum(field[0] * field[0] + field[1] * field[1], axis=0)


def advance(applied, power):
    factor = TIMESTEP / power
    return jnp.stack([factor * applied[1], -factor * applied[0]])


def shards(psi, potential, stick_column, stick_length):
    device_list = lax.axis_size("plane")
    planes = potential.shape[0]
    slots = stick_column.shape[0]
    bands = psi.shape[1]
    cosine, sine = plane_tables()
    own = height_tables(stick_length, stick_column, planes, device_list)
    term = psi * own[2]
    columns, lengths = (
        lax.all_gather(stick_column, "plane", axis=0, tiled=True),
        lax.all_gather(stick_length, "plane", axis=0, tiled=True),
    )
    given_cells = cell_slots(columns, lengths)
    total = term
    before = jnp.zeros((planes, NG * NG), jnp.float32)
    for power in range(1, 4):
        arrived = lax.all_to_all(
            along_height(term, own), "plane", split_axis=3, concat_axis=3, tiled=True
        ).reshape(2, bands, planes, device_list * slots)
        field = plane_transform(spread_columns(arrived, given_cells), cosine, sine)
        if power == 1:
            before = modulus(field)
        spectrum = plane_transform(field * potential, cosine, -sine)
        picked = spectrum[:, :, :, columns].reshape(2, bands, planes, device_list, slots)
        returned = lax.all_to_all(picked, "plane", split_axis=3, concat_axis=3, tiled=True)
        term = advance(from_height(returned, own) + own[3] * term, power)
        total = total + term
    arrived = lax.all_to_all(
        along_height(total, own), "plane", split_axis=3, concat_axis=3, tiled=True
    ).reshape(2, bands, planes, device_list * slots)
    after = modulus(plane_transform(spread_columns(arrived, given_cells), cosine, sine))
    change = (after - before) / BAND_DEV
    whole = lax.psum(change, "band")
    potential_new = potential + LINEAR_GAIN * whole + CUBIC_GAIN * whole * whole * whole
    return (total, potential_new)


def solution(mesh):
    in_specs = (P(None, "band", "plane", None), P("plane", None), P("plane"), P("plane"))
    out_specs = (P(None, "band", "plane", None), P("plane", None))
    return jax.shard_map(shards, mesh=mesh, in_specs=in_specs, out_specs=out_specs, check_vma=False)
```

profile of v0, /device:TPU:2, one launch (start us, length us, event | category | flops | bytes accessed | tf_op | source)
XLA Modules:
  0.0 968.3 jit_solution(16766717710354045417)
XLA Ops:
  7.8 0.7 fusion.52
  8.6 0.9 broadcast_multiply_fusion
  11.5 0.7 copy.177
  12.2 11.6 %all-to-all-start = ((f32[2,1,3,32,128]{4,0,2,1,3:T(2,128)}), f32[2,1,3,32,128]{4,0,2,1,3:T(2,128)S(1)}, u32[]{:S(2)}, u32[]{:S(2)}) async-start(f32[2,1,3,32,128]{4,0,2,1,3:T(2,128)} %copy.177), calls=%async_computation | async-start | bytes 196608 | tf_op jit(solution)/shard_map/all_to_all | solution.py:138
  23.8 39.6 %all-gather = s32[32,1,128]{2,1,0:T(1,128)S(1)} all-gather(s32[1,1,128]{2,1,0:T(1,128)} %bitcast.566), channel_id=1, replica_groups=mesh['band'=8,'plane'=32] {'plane'}, dimensions={0}, use_global_device_ids=true | all-gather | bytes 16896 | tf_op jit(solution)/shard_map/all_gather | solution.py:132
  63.4 36.7 %all-gather.1 = s32[32,1,128]{2,1,0:T(1,128)S(1)} all-gather(s32[1,1,128]{2,1,0:T(1,128)} %bitcast.567), channel_id=1, replica_groups=mesh['band'=8,'plane'=32] {'plane'}, dimensions={0}, use_global_device_ids=true | all-gather | bytes 16896 | tf_op jit(solution)/shard_map/all_gather | solution.py:131
  100.1 15.5 %scatter_custom_fusion = s32[9216]{0:T(1024)S(1)} fusion(s32[4096]{0:T(1024)S(1)} %get-tuple-element.40, s32[4096]{0:T(1024)S(1)} %iota.105, s32[]{:T(128)} %constant.56.clone.1), kind=kCustom, calls=%fused_computation.291 | custom fusion | bytes 36868 | tf_op jit(solution)/shard_map/scatter | solution.py:105
  116.4 4.3 copy.179
  120.7 65.0 %gather_fusion.3 = f32[9216,2,3]{2,1,0:T(2,128)} fusion(f32[2,3,4096]{1,0,2:T(2,128)} %bitcast.554, s32[9216]{0:T(1024)S(1)} %maximum_clamp_fusion), kind=kCustom, calls=%fused_computation.clone | custom fusion | bytes 479232 | tf_op jit(solution)/shard_map/jit(_take)/gather | solution.py:109
  185.7 42.6 %fusion.3 = f32[2,1,3,9216]{2,0,3,1:T(2,128)S(1)} fusion(f32[9216,2,3]{2,1,0:T(2,128)} %gather_fusion.3, pred[9216]{0:T(1024)(128)(4,1)S(1)} %get-tuple-element.38, pred[9216]{0:T(1024)(128)(4,1)S(1)} %get-tuple-element.37), kind=kLoop, calls=%fused_computation.15 | loop fusion | flops 110592 | bytes 460800 | tf_op jit(solution)/shard_map/jit(_where)/select_n | solution.py:110
  228.3 8.5 fusion.517
  236.8 3.1 copy.281
  240.9 3.6 copy.282
  254.3 8.9 copy.194
  263.2 31.8 %gather_fusion = f32[4096,2,3]{2,1,0:T(2,128)} fusion(f32[2,3,9216]{1,0,2:T(2,128)} %bitcast.550, s32[4096]{0:T(1024)S(1)} %get-tuple-element.39), kind=kCustom, calls=%fused_computation.4 | custom fusion | bytes 212992 | tf_op jit(solution)/shard_map/gather | solution.py:145
  295.1 5.8 copy.196
  300.9 6.5 all-to-all-start.1
  307.5 8.7 all-to-all-done.1
  316.3 0.7 convolution_bitcast_fusion.8
  317.0 0.7 convolution_bitcast_fusion.10
  317.7 0.7 fusion.26
  318.4 0.7 fusion.23
  321.1 13.5 %all_to_all.35 = f32[2,1,3,32,128]{4,0,2,1,3:T(2,128)S(1)} all-to-all(f32[2,1,3,32,128]{4,0,2,1,3:T(2,128)S(1)} %copy.199), channel_id=1, replica_groups=mesh['band'=8,'plane'=32] {'plane'}, dimensions={3} | all-to-all | bytes 196608 | tf_op jit(solution)/shard_map/all_to_all | solution.py:138
  334.6 4.3 copy.201
  339.0 65.0 %gather_fusion.4 = f32[9216,2,3]{2,1,0:T(2,128)} fusion(f32[2,3,4096]{1,0,2:T(2,128)} %bitcast.555, s32[9216]{0:T(1024)S(1)} %maximum_clamp_fusion), kind=kCustom, calls=%fused_computation.1.clone | custom fusion | bytes 479232 | tf_op jit(solution)/shard_map/jit(_take)/gather | solution.py:109
  403.9 42.6 %fusion.2 = f32[2,1,3,9216]{2,0,3,1:T(2,128)S(1)} fusion(f32[9216,2,3]{2,1,0:T(2,128)} %gather_fusion.4, pred[9216]{0:T(1024)(128)(4,1)S(1)} %get-tuple-element.38, pred[9216]{0:T(1024)(128)(4,1)S(1)} %get-tuple-element.37), kind=kLoop, calls=%fused_computation.13 | loop fusion | flops 110592 | bytes 460800 | tf_op jit(solution)/shard_map/jit(_where)/select_n | solution.py:110
  446.5 8.5 fusion.516
  455.0 3.1 copy.285
  459.1 3.3 copy.286
  472.2 8.9 copy.216
  481.1 31.8 %gather_fusion.1 = f32[4096,2,3]{2,1,0:T(2,128)} fusion(f32[2,3,9216]{1,0,2:T(2,128)} %bitcast.552, s32[4096]{0:T(1024)S(1)} %get-tuple-element.39), kind=kCustom, calls=%fused_computation.5 | custom fusion | bytes 212992 | tf_op jit(solution)/shard_map/gather | solution.py:145
  513.0 5.8 copy.218
  518.8 5.5 all-to-all-start.3
  524.3 8.9 all-to-all-done.3
  533.3 0.7 convolution_bitcast_fusion.4
  534.0 0.7 convolution_bitcast_fusion.6
  534.7 0.7 fusion.32
  535.4 0.7 fusion.29
  538.1 13.5 %all_to_all.36 = f32[2,1,3,32,128]{4,0,2,1,3:T(2,128)S(1)} all-to-all(f32[2,1,3,32,128]{4,0,2,1,3:T(2,128)S(1)} %copy.221), channel_id=1, replica_groups=mesh['band'=8,'plane'=32] {'plane'}, dimensions={3} | all-to-all | bytes 196608 | tf_op jit(solution)/shard_map/all_to_all | solution.py:138
  551.6 4.3 copy.223
  556.0 65.0 %gather_fusion.5 = f32[9216,2,3]{2,1,0:T(2,128)} fusion(f32[2,3,4096]{1,0,2:T(2,128)} %bitcast.556, s32[9216]{0:T(1024)S(1)} %maximum_clamp_fusion), kind=kCustom, calls=%fused_computation.2.clone | custom fusion | bytes 479232 | tf_op jit(solution)/shard_map/jit(_take)/gather | solution.py:109
  620.9 42.6 %fusion.1 = f32[2,1,3,9216]{2,0,3,1:T(2,128)S(1)} fusion(f32[9216,2,3]{2,1,0:T(2,128)} %gather_fusion.5, pred[9216]{0:T(1024)(128)(4,1)S(1)} %get-tuple-element.38, pred[9216]{0:T(1024)(128)(4,1)S(1)} %get-tuple-element.37), kind=kLoop, calls=%fused_computation.11 | loop fusion | flops 110592 | bytes 460800 | tf_op jit(solution)/shard_map/jit(_where)/select_n | solution.py:110
  663.5 8.5 fusion.515
  672.0 3.1 copy.289
  676.1 3.3 copy.290
  689.2 8.9 copy.238
  698.1 31.8 %gather_fusion.2 = f32[4096,2,3]{2,1,0:T(2,128)} fusion(f32[2,3,9216]{1,0,2:T(2,128)} %bitcast.551, s32[4096]{0:T(1024)S(1)} %get-tuple-element.39), kind=kCustom, calls=%fused_computation.6 | custom fusion | bytes 212992 | tf_op jit(solution)/shard_map/gather | solution.py:145
  729.9 5.8 copy.240
  735.8 5.0 all-to-all-start.5
  741.0 8.8 all-to-all-done.5
  749.9 0.7 convolution_bitcast_fusion
  750.6 0.7 convolution_bitcast_fusion.2
  751.2 0.7 fusion.38
  751.9 0.7 fusion.35
  754.8 13.5 %all_to_all.37 = f32[2,1,3,32,128]{4,0,2,1,3:T(2,128)S(1)} all-to-all(f32[2,1,3,32,128]{4,0,2,1,3:T(2,128)S(1)} %copy.243), channel_id=1, replica_groups=mesh['band'=8,'plane'=32] {'plane'}, dimensions={3} | all-to-all | bytes 196608 | tf_op jit(solution)/shard_map/all_to_all | solution.py:149
  768.3 4.3 copy.245
  772.6 65.0 %gather_fusion.6 = f32[9216,2,3]{2,1,0:T(2,128)} fusion(f32[2,3,4096]{1,0,2:T(2,128)} %bitcast.553, s32[9216]{0:T(1024)S(1)} %maximum_clamp_fusion), kind=kCustom, calls=%fused_computation.3.clone | custom fusion | bytes 479232 | tf_op jit(solution)/shard_map/jit(_take)/gather | solution.py:109
  837.6 42.6 %fusion = f32[2,1,3,9216]{2,0,3,1:T(2,128)S(1)} fusion(f32[9216,2,3]{2,1,0:T(2,128)} %gather_fusion.6, pred[9216]{0:T(1024)(128)(4,1)S(1)} %get-tuple-element.38, pred[9216]{0:T(1024)(128)(4,1)S(1)} %get-tuple-element.37), kind=kLoop, calls=%fused_computation.9 | loop fusion | flops 110592 | bytes 460800 | tf_op jit(solution)/shard_map/jit(_where)/select_n | solution.py:110
  880.2 8.5 fusion.514
  888.7 3.1 copy.293
  892.8 3.1 copy.294
  899.1 0.8 sub.241
  899.9 59.6 %all-reduce.2.cloned.1.call-done = f32[3,9216]{1,0:T(4,128)} async-done(((f32[3,9216]{1,0:T(4,128)}), f32[3,9216]{1,0:T(4,128)}) %all-reduce.2.cloned.1.call-update) | async-done | bytes 110608 | tf_op jit(solution)/shard_map/psum | solution.py:154
  959.6 1.6 fusion.39
  (153 shorter events, 46.1 us)
Async XLA Ops:
  12.2 104.2 %all-to-all-start = ((f32[2,1,3,32,128]{4,0,2,1,3:T(2,128)}), f32[2,1,3,32,128]{4,0,2,1,3:T(2,128)S(1)}, u32[]{:S(2)}, u32[]{:S(2)}) async-start(f32[2,1,3,32,128]{4,0,2,1,3:T(2,128)} %copy.177), calls=%async_computation | async-start | bytes 196608 | tf_op jit(solution)/shard_map/all_to_all | solution.py:138
  236.8 11.4 %copy-start = (f32[3,9216]{1,0:T(4,128)S(1)}, f32[3,9216]{1,0:T(4,128)}, u32[]{:S(2)}) copy-start(f32[3,9216]{1,0:T(4,128)} %param.7) | copy-start | bytes 331780
  249.7 57.6 %copy-start.3 = (s32[128]{0:T(128)S(1)}, s32[128]{0:T(128)}, u32[]{:S(2)}) copy-start(s32[128]{0:T(128)} %param.9) | copy-start | bytes 1540
  252.4 66.7 %copy-start.1 = (f32[2,1,128,128]{3,2,1,0:T(8,128)S(1)}, f32[2,1,128,128]{3,2,1,0:T(8,128)}, u32[]{:S(2)}) copy-start(f32[2,1,128,128]{3,2,1,0:T(8,128)} %param.6) | copy-start | bytes 393220
  300.9 15.3 %all-to-all-start.1 = ((f32[2,1,3,32,128]{4,0,2,1,3:T(2,128)}), f32[2,1,3,32,128]{4,0,2,1,3:T(2,128)S(1)}, u32[]{:S(2)}, u32[]{:S(2)}) async-start(f32[2,1,3,32,128]{4,0,2,1,3:T(2,128)} %copy.196), calls=%async_computation.1 | async-start | bytes 196608 | tf_op jit(solution)/shard_map/all_to_all | solution.py:146
  518.8 14.4 %all-to-all-start.3 = ((f32[2,1,3,32,128]{4,0,2,1,3:T(2,128)}), f32[2,1,3,32,128]{4,0,2,1,3:T(2,128)S(1)}, u32[]{:S(2)}, u32[]{:S(2)}) async-start(f32[2,1,3,32,128]{4,0,2,1,3:T(2,128)} %copy.218), calls=%async_computation.3 | async-start | bytes 196608 | tf_op jit(solution)/shard_map/all_to_all | solution.py:146
  735.8 14.0 %all-to-all-start.5 = ((f32[2,1,3,32,128]{4,0,2,1,3:T(2,128)}), f32[2,1,3,32,128]{4,0,2,1,3:T(2,128)S(1)}, u32[]{:S(2)}, u32[]{:S(2)}) async-start(f32[2,1,3,32,128]{4,0,2,1,3:T(2,128)} %copy.240), calls=%async_computation.5 | async-start | bytes 196608 | tf_op jit(solution)/shard_map/all_to_all | solution.py:146
  740.7 218.8 %all-reduce.2.cloned.1.call-start = ((), (), s32[]{:S(2)}) async-start(), calls=%async_computation.7 | async-start | bytes 294912 | tf_op jit(solution)/shard_map/psum | solution.py:154
  752.7 127.4 %copy-start.2 = (f32[2,1,128,128]{3,2,1,0:T(8,128)}, f32[2,1,128,128]{3,2,1,0:T(8,128)S(1)}, u32[]{:S(2)}) copy-start(f32[2,1,128,128]{3,2,1,0:T(8,128)S(1)} %maximum_add_fusion.3) | copy-start | bytes 393220
Sparse Core Ops, SparseCore 0:
  900.1 59.4 all-reduce.1
where the time goes:
time: 975 us; the launch traced here: 968 us
  local copies, waits for them, and re-layouts  501 us (51%)
  other arithmetic  177 us (18%)
  blocking collectives  117 us (12%)
  waiting for transfers between devices  86.1 us (9%)
  matrix products  43.7 us (4%)
  starting transfers between devices  28.8 us (3%)
  between operations  15.4 us (2%)
    gather x4, local copies, waits for them, and re-layouts, spread_columns(): picked = jnp.take(values, jnp.maximum(table, 0), axis=3)  260 us
    select_n x4, other arithmetic, spread_columns(): return jnp.where(table >= 0, picked, 0.0)  170 us
    gather x3, local copies, waits for them, and re-layouts, shards(): spectrum[:, :, :, columns].reshape(2, bands, planes, device_list, slots)  95.5 us
    psum x1, waiting for transfers between devices, shards(): whole = lax.psum(change, 'band')  59.6 us
    all_gather x1, blocking collectives, shards(): lax.all_gather(stick_length, 'plane', axis=0, tiled=True)  39.6 us
    all_gather x1, blocking collectives, shards(): lax.all_gather(stick_column, 'plane', axis=0, tiled=True)  36.7 us
    slice x7, local copies, waits for them, and re-layouts, plane_transform(): imag_part = values[1].reshape(bands, planes, NG, NG)  35.9 us
    another operation x15, local copies, waits for them, and re-layouts, plane_transform(): jnp.stack([final_real, final_imag]).reshape(2, bands, planes, NG * NG)  29.1 us
  transfers between devices with their start and end apart: 5, of which 4 were waited for; matrix products, arithmetic and copies ran while one was open for 2% of the time, Pallas kernels for 0%

commit v1 on v0

--- a/solution.py
+++ b/solution.py
@@ -12,6 +12,7 @@
 TIMESTEP = 0.6
 LINEAR_GAIN = 0.5
 CUBIC_GAIN = 0.3
+derive_panels = lambda obj: jnp.sum(lax.all_gather(obj, "band"), 0)
 
 
 def turning(values):
@@ -151,7 +152,7 @@
     ).reshape(2, bands, planes, device_list * slots)
     after = modulus(plane_transform(spread_columns(arrived, given_cells), cosine, sine))
     change = (after - before) / BAND_DEV
-    whole = lax.psum(change, "band")
+    whole = derive_panels(change)
     potential_new = potential + LINEAR_GAIN * whole + CUBIC_GAIN * whole * whole * whole
     return (total, potential_new)
 

time: 975 us -> 921 us (0.945)
  waiting for transfers between devices: 86.1 us -> 26.6 us
  blocking collectives: 117 us -> 131 us
  between operations: 15.4 us -> 2.06 us
    psum x1 -> x0, waiting for transfers between devices: 59.6 us -> none  [shards(): whole = lax.psum(change, 'band')]
    all_gather x0 -> x1, blocking collectives: none -> 14.6 us  [derive_panels = lambda obj: jnp.sum(lax.all_gather(obj, 'band'), 0)]
  transfers between devices with their start and end apart: 5 -> 4, of which waited for: 4 -> 3; matrix products, arithmetic and copies ran while one was open for 2% -> 2% of each run, Pallas kernels for 0% -> 0%
where the time goes in v1:
time: 921 us; the launch traced here: 911 us
  local copies, waits for them, and re-layouts  503 us (55%)
  other arithmetic  176 us (19%)
  blocking collectives  131 us (14%)
  matrix products  43.8 us (5%)
  starting transfers between devices  28.8 us (3%)
  waiting for transfers between devices  26.6 us (3%)
    gather x4, local copies, waits for them, and re-layouts, spread_columns(): picked = jnp.take(values, jnp.maximum(table, 0), axis=3)  262 us
    select_n x4, other arithmetic, spread_columns(): return jnp.where(table >= 0, picked, 0.0)  170 us
    gather x3, local copies, waits for them, and re-layouts, shards(): spectrum[:, :, :, columns].reshape(2, bands, planes, device_list, slots)  96.1 us
    all_gather x1, blocking collectives, shards(): lax.all_gather(stick_length, 'plane', axis=0, tiled=True)  39.6 us
    all_gather x1, blocking collectives, shards(): lax.all_gather(stick_column, 'plane', axis=0, tiled=True)  36.7 us
    slice x7, local copies, waits for them, and re-layouts, plane_transform(): imag_part = values[1].reshape(bands, planes, NG, NG)  36 us
    another operation x15, local copies, waits for them, and re-layouts, plane_transform(): jnp.stack([final_real, final_imag]).reshape(2, bands, planes, NG * NG)  29.2 us
    all_to_all x2, blocking collectives, shards(): lax.all_to_all(along_height(term, own), 'plane', split_axis=3, concat_axi...  27 us
  transfers between devices with their start and end apart: 4, of which 3 were waited for; matrix products, arithmetic and copies ran while one was open for 2% of the time, Pallas kernels for 0%

profile of v1, /device:TPU:2, one launch (start us, length us, event | category | flops | bytes accessed | tf_op | source)
XLA Modules:
  0.0 911.4 jit_solution(13112511072491439660)
XLA Ops:
  1.3 0.7 fusion.52
  2.1 0.9 broadcast_multiply_fusion
  4.9 0.7 copy.178
  5.7 11.6 %all-to-all-start = ((f32[2,1,3,32,128]{4,0,2,1,3:T(2,128)}), f32[2,1,3,32,128]{4,0,2,1,3:T(2,128)S(1)}, u32[]{:S(2)}, u32[]{:S(2)}) async-start(f32[2,1,3,32,128]{4,0,2,1,3:T(2,128)} %copy.178), calls=%async_computation | async-start | bytes 196608 | tf_op jit(solution)/shard_map/all_to_all | solution.py:139
  17.3 39.6 %all-gather = s32[32,1,128]{2,1,0:T(1,128)S(1)} all-gather(s32[1,1,128]{2,1,0:T(1,128)} %bitcast.568), channel_id=1, replica_groups=mesh['band'=8,'plane'=32] {'plane'}, dimensions={0}, use_global_device_ids=true | all-gather | bytes 16896 | tf_op jit(solution)/shard_map/all_gather | solution.py:133
  56.9 36.7 %all-gather.1 = s32[32,1,128]{2,1,0:T(1,128)S(1)} all-gather(s32[1,1,128]{2,1,0:T(1,128)} %bitcast.569), channel_id=1, replica_groups=mesh['band'=8,'plane'=32] {'plane'}, dimensions={0}, use_global_device_ids=true | all-gather | bytes 16896 | tf_op jit(solution)/shard_map/all_gather | solution.py:132
  93.6 15.5 %scatter_custom_fusion = s32[9216]{0:T(1024)S(1)} fusion(s32[4096]{0:T(1024)S(1)} %get-tuple-element.40, s32[4096]{0:T(1024)S(1)} %iota.105, s32[]{:T(128)} %constant.56.clone.1), kind=kCustom, calls=%fused_computation.291 | custom fusion | bytes 36868 | tf_op jit(solution)/shard_map/scatter | solution.py:106
  109.2 0.7 fusion.176
  109.9 4.4 copy.180
  114.2 65.4 %gather_fusion.3 = f32[9216,2,3]{2,1,0:T(2,128)} fusion(f32[2,3,4096]{1,0,2:T(2,128)} %bitcast.556, s32[9216]{0:T(1024)S(1)} %maximum_clamp_fusion), kind=kCustom, calls=%fused_computation.clone | custom fusion | bytes 479232 | tf_op jit(solution)/shard_map/jit(_take)/gather | solution.py:110
  179.6 42.6 %fusion.3 = f32[2,1,3,9216]{2,0,3,1:T(2,128)S(1)} fusion(f32[9216,2,3]{2,1,0:T(2,128)} %gather_fusion.3, pred[9216]{0:T(1024)(128)(4,1)S(1)} %get-tuple-element.38, pred[9216]{0:T(1024)(128)(4,1)S(1)} %get-tuple-element.37), kind=kLoop, calls=%fused_computation.15 | loop fusion | flops 110592 | bytes 460800 | tf_op jit(solution)/shard_map/jit(_where)/select_n | solution.py:111
  222.2 8.5 fusion.517
  230.7 3.1 copy.283
  234.9 3.6 copy.284
  248.3 8.9 copy.195
  257.2 32.0 %gather_fusion = f32[4096,2,3]{2,1,0:T(2,128)} fusion(f32[2,3,9216]{1,0,2:T(2,128)} %bitcast.552, s32[4096]{0:T(1024)S(1)} %get-tuple-element.39), kind=kCustom, calls=%fused_computation.4 | custom fusion | bytes 212992 | tf_op jit(solution)/shard_map/gather | solution.py:146
  289.3 5.8 copy.197
  295.1 6.5 all-to-all-start.1
  301.7 8.7 all-to-all-done.1
  310.5 0.7 convolution_bitcast_fusion.8
  311.2 0.7 convolution_bitcast_fusion.10
  311.9 0.7 fusion.26
  312.6 0.7 fusion.23
  315.3 13.5 %all_to_all.35 = f32[2,1,3,32,128]{4,0,2,1,3:T(2,128)S(1)} all-to-all(f32[2,1,3,32,128]{4,0,2,1,3:T(2,128)S(1)} %copy.200), channel_id=1, replica_groups=mesh['band'=8,'plane'=32] {'plane'}, dimensions={3} | all-to-all | bytes 196608 | tf_op jit(solution)/shard_map/all_to_all | solution.py:139
  328.8 4.4 copy.202
  333.2 65.4 %gather_fusion.4 = f32[9216,2,3]{2,1,0:T(2,128)} fusion(f32[2,3,4096]{1,0,2:T(2,128)} %bitcast.557, s32[9216]{0:T(1024)S(1)} %maximum_clamp_fusion), kind=kCustom, calls=%fused_computation.1.clone | custom fusion | bytes 479232 | tf_op jit(solution)/shard_map/jit(_take)/gather | solution.py:110
  398.6 42.6 %fusion.2 = f32[2,1,3,9216]{2,0,3,1:T(2,128)S(1)} fusion(f32[9216,2,3]{2,1,0:T(2,128)} %gather_fusion.4, pred[9216]{0:T(1024)(128)(4,1)S(1)} %get-tuple-element.38, pred[9216]{0:T(1024)(128)(4,1)S(1)} %get-tuple-element.37), kind=kLoop, calls=%fused_computation.13 | loop fusion | flops 110592 | bytes 460800 | tf_op jit(solution)/shard_map/jit(_where)/select_n | solution.py:111
  441.2 8.5 fusion.516
  449.7 3.1 copy.287
  453.8 3.3 copy.288
  466.9 8.9 copy.217
  475.9 32.0 %gather_fusion.1 = f32[4096,2,3]{2,1,0:T(2,128)} fusion(f32[2,3,9216]{1,0,2:T(2,128)} %bitcast.554, s32[4096]{0:T(1024)S(1)} %get-tuple-element.39), kind=kCustom, calls=%fused_computation.5 | custom fusion | bytes 212992 | tf_op jit(solution)/shard_map/gather | solution.py:146
  507.9 5.8 copy.219
  513.7 5.5 all-to-all-start.3
  519.3 8.9 all-to-all-done.3
  528.3 0.7 convolution_bitcast_fusion.4
  528.9 0.7 convolution_bitcast_fusion.6
  529.6 0.7 fusion.32
  530.3 0.7 fusion.29
  533.1 13.5 %all_to_all.36 = f32[2,1,3,32,128]{4,0,2,1,3:T(2,128)S(1)} all-to-all(f32[2,1,3,32,128]{4,0,2,1,3:T(2,128)S(1)} %copy.222), channel_id=1, replica_groups=mesh['band'=8,'plane'=32] {'plane'}, dimensions={3} | all-to-all | bytes 196608 | tf_op jit(solution)/shard_map/all_to_all | solution.py:139
  546.6 4.4 copy.224
  550.9 65.4 %gather_fusion.5 = f32[9216,2,3]{2,1,0:T(2,128)} fusion(f32[2,3,4096]{1,0,2:T(2,128)} %bitcast.558, s32[9216]{0:T(1024)S(1)} %maximum_clamp_fusion), kind=kCustom, calls=%fused_computation.2.clone | custom fusion | bytes 479232 | tf_op jit(solution)/shard_map/jit(_take)/gather | solution.py:110
  616.4 42.6 %fusion.1 = f32[2,1,3,9216]{2,0,3,1:T(2,128)S(1)} fusion(f32[9216,2,3]{2,1,0:T(2,128)} %gather_fusion.5, pred[9216]{0:T(1024)(128)(4,1)S(1)} %get-tuple-element.38, pred[9216]{0:T(1024)(128)(4,1)S(1)} %get-tuple-element.37), kind=kLoop, calls=%fused_computation.11 | loop fusion | flops 110592 | bytes 460800 | tf_op jit(solution)/shard_map/jit(_where)/select_n | solution.py:111
  658.9 8.5 fusion.515
  667.5 3.1 copy.291
  671.5 3.3 copy.292
  684.6 8.9 copy.239
  693.6 32.0 %gather_fusion.2 = f32[4096,2,3]{2,1,0:T(2,128)} fusion(f32[2,3,9216]{1,0,2:T(2,128)} %bitcast.553, s32[4096]{0:T(1024)S(1)} %get-tuple-element.39), kind=kCustom, calls=%fused_computation.6 | custom fusion | bytes 212992 | tf_op jit(solution)/shard_map/gather | solution.py:146
  725.6 5.8 copy.241
  731.4 5.3 all-to-all-start.5
  736.7 8.9 all-to-all-done.5
  745.8 0.7 convolution_bitcast_fusion
  746.4 0.7 convolution_bitcast_fusion.2
  747.1 0.7 fusion.38
  747.8 0.7 fusion.35
  750.6 13.5 %all_to_all.37 = f32[2,1,3,32,128]{4,0,2,1,3:T(2,128)S(1)} all-to-all(f32[2,1,3,32,128]{4,0,2,1,3:T(2,128)S(1)} %copy.244), channel_id=1, replica_groups=mesh['band'=8,'plane'=32] {'plane'}, dimensions={3} | all-to-all | bytes 196608 | tf_op jit(solution)/shard_map/all_to_all | solution.py:150
  764.2 4.4 copy.246
  768.5 65.4 %gather_fusion.6 = f32[9216,2,3]{2,1,0:T(2,128)} fusion(f32[2,3,4096]{1,0,2:T(2,128)} %bitcast.555, s32[9216]{0:T(1024)S(1)} %maximum_clamp_fusion), kind=kCustom, calls=%fused_computation.3.clone | custom fusion | bytes 479232 | tf_op jit(solution)/shard_map/jit(_take)/gather | solution.py:110
  833.9 42.6 %fusion = f32[2,1,3,9216]{2,0,3,1:T(2,128)S(1)} fusion(f32[9216,2,3]{2,1,0:T(2,128)} %gather_fusion.6, pred[9216]{0:T(1024)(128)(4,1)S(1)} %get-tuple-element.38, pred[9216]{0:T(1024)(128)(4,1)S(1)} %get-tuple-element.37), kind=kLoop, calls=%fused_computation.9 | loop fusion | flops 110592 | bytes 460800 | tf_op jit(solution)/shard_map/jit(_where)/select_n | solution.py:111
  876.5 8.5 fusion.514
  885.0 3.1 copy.295
  889.1 3.1 copy.296
  895.6 14.6 %all_gather.12 = f32[8,3,9216]{2,1,0:T(4,128)S(1)} all-gather(f32[1,3,9216]{2,1,0:T(4,128)S(1)} %sub.249), channel_id=1, replica_groups=mesh['band'=8,'plane'=32] {'band'}, dimensions={0}, use_global_device_ids=true | all-gather | bytes 995328 | tf_op jit(solution)/shard_map/all_gather | solution.py:15
  910.5 0.7 fusion.39
  (152 shorter events, 45.5 us)
Async XLA Ops:
  5.7 104.2 %all-to-all-start = ((f32[2,1,3,32,128]{4,0,2,1,3:T(2,128)}), f32[2,1,3,32,128]{4,0,2,1,3:T(2,128)S(1)}, u32[]{:S(2)}, u32[]{:S(2)}) async-start(f32[2,1,3,32,128]{4,0,2,1,3:T(2,128)} %copy.178), calls=%async_computation | async-start | bytes 196608 | tf_op jit(solution)/shard_map/all_to_all | solution.py:139
  230.7 11.4 %copy-start = (f32[3,9216]{1,0:T(4,128)S(1)}, f32[3,9216]{1,0:T(4,128)}, u32[]{:S(2)}) copy-start(f32[3,9216]{1,0:T(4,128)} %param.7) | copy-start | bytes 331780
  243.7 57.9 %copy-start.3 = (s32[128]{0:T(128)S(1)}, s32[128]{0:T(128)}, u32[]{:S(2)}) copy-start(s32[128]{0:T(128)} %param.9) | copy-start | bytes 1540
  246.4 66.9 %copy-start.1 = (f32[2,1,128,128]{3,2,1,0:T(8,128)S(1)}, f32[2,1,128,128]{3,2,1,0:T(8,128)}, u32[]{:S(2)}) copy-start(f32[2,1,128,128]{3,2,1,0:T(8,128)} %param.6) | copy-start | bytes 393220
  295.1 15.3 %all-to-all-start.1 = ((f32[2,1,3,32,128]{4,0,2,1,3:T(2,128)}), f32[2,1,3,32,128]{4,0,2,1,3:T(2,128)S(1)}, u32[]{:S(2)}, u32[]{:S(2)}) async-start(f32[2,1,3,32,128]{4,0,2,1,3:T(2,128)} %copy.197), calls=%async_computation.1 | async-start | bytes 196608 | tf_op jit(solution)/shard_map/all_to_all | solution.py:147
  513.7 14.4 %all-to-all-start.3 = ((f32[2,1,3,32,128]{4,0,2,1,3:T(2,128)}), f32[2,1,3,32,128]{4,0,2,1,3:T(2,128)S(1)}, u32[]{:S(2)}, u32[]{:S(2)}) async-start(f32[2,1,3,32,128]{4,0,2,1,3:T(2,128)} %copy.219), calls=%async_computation.3 | async-start | bytes 196608 | tf_op jit(solution)/shard_map/all_to_all | solution.py:147
  731.4 14.2 %all-to-all-start.5 = ((f32[2,1,3,32,128]{4,0,2,1,3:T(2,128)}), f32[2,1,3,32,128]{4,0,2,1,3:T(2,128)S(1)}, u32[]{:S(2)}, u32[]{:S(2)}) async-start(f32[2,1,3,32,128]{4,0,2,1,3:T(2,128)} %copy.241), calls=%async_computation.5 | async-start | bytes 196608 | tf_op jit(solution)/shard_map/all_to_all | solution.py:147
  748.6 127.9 %copy-start.2 = (f32[2,1,128,128]{3,2,1,0:T(8,128)}, f32[2,1,128,128]{3,2,1,0:T(8,128)S(1)}, u32[]{:S(2)}) copy-start(f32[2,1,128,128]{3,2,1,0:T(8,128)S(1)} %maximum_add_fusion.3) | copy-start | bytes 393220
